TPU v7x, 256 devices: a whole 4x4x8 slice. The times are simulated.
256 devices in a mesh: row: 8 (over x, y_hi), col: 32 (over y_lo, z, core).
Axes of the slice: x: 4, y: 4 (y_hi: 2, y_lo: 2; y = y_hi * 2 + y_lo), z: 8, core: 2. Of those that a mesh axis runs over, the one named last changes fastest.
Arguments:
- embed: float32 [65536, 128], P(('row', 'col')), may hold values from -6 to 6
- cotangent: float32 [65536, 128], P(('col', 'row')), may hold values from -6 to 6
- tile_values: float32 [32, 8, 128, 128, 128], P('col', 'row'), may hold values from 0 to 1
- tile_coords: int32 [2, 32, 8, 128], P(None, 'col', 'row'), may hold values from 0 to 63, as said below
- tile_count: int32 [32, 8], P('col', 'row'), may hold values from 1 to 128, as said below
- row_degree: int32 [65536], P(('col', 'row')), may hold values from 16 to 511
- col_degree: int32 [65536], P(('row', 'col')), may hold values from 16 to 511
Outputs:
- propagated: float32 [65536, 128], P(('col', 'row'))
- embed_grad: float32 [65536, 128], P(('row', 'col'))
Inputs may be any that keep to these rules, and one draw needn't show every extreme that they name: `tile_coords`: within one device block the slots hold distinct tile positions; the first component is below 16 and the second below 64. `tile_count`: some device block has all 128 slots live.
All inputs are finite; a program needn't handle non-finite values.
Results may differ from a plain program's by a relative error of at most 0.0003.
Values sent between devices are 32-bit elements; how exact they have to be, the bound alone decides.
A program may use at most 128 MiB of HBM per device.

v0:
```python
import jax
import jax.numpy as jnp
from jax import lax
from jax.sharding import PartitionSpec as P


def tile_terms(values, rows_at, cols_at, live_mask, panel_tiles, grad_tiles):
    picked = jnp.take(panel_tiles, cols_at, axis=0)
    forward_each = jnp.einsum("tij,tjd->tid", values, picked, precision=lax.Precision.HIGHEST)
    row_hot = (
        (rows_at[None, :] == jnp.arange(grad_tiles.shape[0], dtype=jnp.int32)[:, None])
        & live_mask[None, :]
    ).astype(jnp.float32)
    forward = jnp.einsum("at,tid->aid", row_hot, forward_each, precision=lax.Precision.HIGHEST)
    grad_picked = jnp.take(grad_tiles, rows_at, axis=0)
    backward_each = jnp.einsum("tij,tid->tjd", values, grad_picked, precision=lax.Precision.HIGHEST)
    col_hot = (
        (cols_at[None, :] == jnp.arange(panel_tiles.shape[0], dtype=jnp.int32)[:, None])
        & live_mask[None, :]
    ).astype(jnp.float32)
    backward = jnp.einsum("bt,tjd->bjd", col_hot, backward_each, precision=lax.Precision.HIGHEST)
    return (forward, backward)


def per_device(embed, cotangent, tile_values, tile_coords, tile_count, row_degree, col_degree):
    tile_size = tile_values.shape[-1]
    feature_width = embed.shape[1]
    capacity = tile_values.shape[2]
    values = tile_values[0, 0]
    rows_at = tile_coords[0, 0, 0]
    cols_at = tile_coords[1, 0, 0]
    live_count = tile_count[0, 0]
    scaled = embed * lax.rsqrt(col_degree.astype(jnp.float32))[:, None]
    grad_scaled = cotangent * lax.rsqrt(row_degree.astype(jnp.float32))[:, None]
    embed_panel = lax.all_gather(scaled, "col", axis=0, tiled=True)
    grad_panel = lax.all_gather(grad_scaled, "row", axis=0, tiled=True)
    panel_tiles = embed_panel.reshape(-1, tile_size, feature_width)
    grad_tiles = grad_panel.reshape(-1, tile_size, feature_width)
    live_mask = jnp.arange(capacity, dtype=jnp.int32) < live_count
    forward, backward = tile_terms(values, rows_at, cols_at, live_mask, panel_tiles, grad_tiles)
    summed = lax.psum_scatter(
        forward.reshape(-1, feature_width), "row", scatter_dimension=0, tiled=True
    )
    propagated = summed * lax.rsqrt(row_degree.astype(jnp.float32))[:, None]
    grad_summed = lax.psum_scatter(
        backward.reshape(-1, feature_width), "col", scatter_dimension=0, tiled=True
    )
    embed_grad = grad_summed * lax.rsqrt(col_degree.astype(jnp.float32))[:, None]
    return (propagated, embed_grad)


def solution(mesh):
    return jax.shard_map(
        per_device,
        mesh=mesh,
        in_specs=(
            P(("row", "col"), None),
            P(("col", "row"), None),
            P("col", "row", None, None, None),
            P(None, "col", "row", None),
            P("col", "row"),
            P(("col", "row")),
            P(("row", "col")),
        ),
        out_specs=(P(("col", "row"), None), P(("row", "col"), None)),
        check_vma=False,
    )
```

profile of v0, /device:TPU:2, one launch (start us, length us, event | category | flops | bytes accessed | tf_op | source)
XLA Modules:
  0.0 428.2 jit_solution(3082143181208052741)
XLA Ops:
  7.2 0.0 all-gather.5.cloned.1.call-start
  7.2 0.7 convert_rsqrt_fusion
  7.9 1.7 broadcast_multiply_fusion
  9.6 0.0 all-gather.5.cloned.1.call-update
  9.6 0.0 reduce-scatter.5.cloned.1.call-start
  10.3 0.7 fusion.25
  11.0 0.7 slice_bitcast_fusion
  11.7 0.7 compare_and_fusion
  12.3 53.9 %all-gather.5.cloned.1.call-done = f32[2048,128]{1,0:T(8,128)} async-done(((f32[256,128]{1,0:T(8,128)}), f32[2048,128]{1,0:T(8,128)}) %all-gather.5.cloned.1.call-update) | async-done | bytes 1048592 | tf_op jit(solution)/shard_map/all_gather | solution.py:36
  66.3 5.5 %gather_fusion.1 = f32[128,128,128]{2,1,0:T(8,128)} fusion(f32[16,128,128]{2,1,0:T(8,128)} %bitcast.39, s32[1024]{0:T(1024)S(1)} %pad_clamp_fusion), kind=kCustom, calls=%fused_computation.1 | custom fusion | bytes 16777728 | tf_op jit(solution)/shard_map/jit(_take)/gather | solution.py:15
  71.8 19.5 %fusion.4 = f32[128,128,128]{2,1,0:T(8,128)} fusion(f32[1,1,128,128,128]{4,3,2,1,0:T(8,128)} %param.9, f32[128,128,128]{2,1,0:T(8,128)} %gather_fusion.1, pred[128]{0:T(512)(128)(4,1)S(1)} %get-tuple-element.6), kind=kOutput, calls=%fused_computation.6 | convolution fusion | flops 3223322624 | bytes 25165952 | tf_op jit(solution)/shard_map/tij,tid->tjd/dot_general | solution.py:16
  91.2 9.4 %copy.12 = f32[128,128,128]{1,0,2:T(8,128)} copy(f32[128,128,128]{2,1,0:T(8,128)} %fusion.4) | data formatting | bytes 16777216 | tf_op jit(solution)/shard_map/tij,tid->tjd/dot_general | solution.py:16
  100.6 6.0 %fusion = f32[64,128,128]{2,0,1:T(8,128)S(1)} fusion(f32[128,128,128]{1,0,2:T(8,128)} %copy.12, s32[128]{0:T(128)S(1)} %get-tuple-element.4, pred[128]{0:T(512)(128)(4,1)S(1)} %iota_compare_fusion.2), kind=kOutput, calls=%fused_computation.2 | convolution fusion | flops 1610629120 | bytes 12583552 | tf_op jit(solution)/shard_map/bt,tjd->bjd/dot_general | solution.py:21
  106.6 0.0 copy-start.1
  106.6 0.0 copy-start
  106.7 4.4 %copy.10 = f32[64,128,128]{2,1,0:T(8,128)} copy(f32[64,128,128]{2,0,1:T(8,128)S(1)} %fusion) | data formatting | bytes 8388608 | tf_op jit(solution)/shard_map/bt,tjd->bjd/dot_general | solution.py:21
  111.0 0.0 reduce-scatter.5.cloned.1.call-update
  111.1 0.0 all-gather.3.cloned.1.call-start
  111.1 0.0 copy-done.1
  111.1 122.8 %reduce-scatter.5.cloned.1.call-done = f32[256,128]{1,0:T(8,128)} async-done(((f32[8192,128]{1,0:T(8,128)}), f32[256,128]{1,0:T(8,128)}) %reduce-scatter.5.cloned.1.call-update) | async-done | bytes 131088 | tf_op jit(solution)/shard_map/reduce_scatter | solution.py:45
  233.9 0.0 copy-done
  233.9 1.7 broadcast_multiply_fusion.2
  235.6 0.0 all-gather.3.cloned.1.call-update
  235.7 0.0 reduce-scatter.3.cloned.1.call-start
  235.7 62.9 %all-gather.3.cloned.1.call-done = f32[8192,128]{1,0:T(8,128)} async-done(((f32[256,128]{1,0:T(8,128)}), f32[8192,128]{1,0:T(8,128)}) %all-gather.3.cloned.1.call-update) | async-done | bytes 4194320 | tf_op jit(solution)/shard_map/all_gather | solution.py:35
  298.6 6.5 %gather_fusion = f32[128,128,128]{2,1,0:T(8,128)} fusion(f32[64,128,128]{2,1,0:T(8,128)} %bitcast.40, s32[1024]{0:T(1024)S(1)} %pad_clamp_fusion.1), kind=kCustom, calls=%fused_computation | custom fusion | bytes 16777728 | tf_op jit(solution)/shard_map/jit(_take)/gather | solution.py:8
  305.1 21.2 %fusion.6 = f32[128,128,128]{2,1,0:T(8,128)} fusion(f32[1,1,128,128,128]{4,3,2,1,0:T(8,128)} %param.9, f32[128,128,128]{2,1,0:T(8,128)} %gather_fusion, pred[128]{0:T(512)(128)(4,1)S(1)} %get-tuple-element.7), kind=kOutput, calls=%fused_computation.8 | convolution fusion | flops 3223322624 | bytes 25165952 | tf_op jit(solution)/shard_map/tij,tjd->tid/dot_general | solution.py:9
  326.3 9.4 %copy.11 = f32[128,128,128]{1,0,2:T(8,128)} copy(f32[128,128,128]{2,1,0:T(8,128)} %fusion.6) | data formatting | bytes 16777216 | tf_op jit(solution)/shard_map/tij,tjd->tid/dot_general | solution.py:9
  335.6 5.2 %fusion.2 = f32[16,128,128]{2,0,1:T(8,128)S(1)} fusion(f32[128,128,128]{1,0,2:T(8,128)} %copy.11, s32[128]{0:T(128)S(1)} %get-tuple-element.5, pred[128]{0:T(512)(128)(4,1)S(1)} %iota_compare_fusion.2), kind=kOutput, calls=%fused_computation.4 | convolution fusion | flops 402657280 | bytes 9437824 | tf_op jit(solution)/shard_map/at,tid->aid/dot_general | solution.py:14
  340.8 1.3 copy.9
  342.1 0.0 reduce-scatter.3.cloned.1.call-update
  342.1 77.9 %reduce-scatter.3.cloned.1.call-done = f32[256,128]{1,0:T(8,128)} async-done(((f32[2048,128]{1,0:T(8,128)}), f32[256,128]{1,0:T(8,128)}) %reduce-scatter.3.cloned.1.call-update) | async-done | bytes 131088 | tf_op jit(solution)/shard_map/reduce_scatter | solution.py:41
  420.0 1.7 broadcast_multiply_fusion.1
  (4 shorter events, 0.0 us)
Async XLA Ops:
  7.2 59.1 %all-gather.5.cloned.1.call-start = ((), (), s32[]{:S(2)}) async-start(), calls=%async_computation.4 | async-start | bytes 1179648 | tf_op jit(solution)/shard_map/all_gather | solution.py:36
  9.6 224.4 %reduce-scatter.5.cloned.1.call-start = ((), (), s32[]{:S(2)}) async-start(), calls=%async_computation.5 | async-start | bytes 4325376 | tf_op jit(solution)/shard_map/reduce_scatter | solution.py:45
  106.6 4.5 %copy-start.1 = (s32[256]{0:T(256)S(1)}, s32[256]{0:T(256)}, u32[]{:S(2)}) copy-start(s32[256]{0:T(256)} %param.13) | copy-start | bytes 3076
  106.6 127.3 %copy-start = (f32[256,128]{1,0:T(8,128)S(1)}, f32[256,128]{1,0:T(8,128)}, u32[]{:S(2)}) copy-start(f32[256,128]{1,0:T(8,128)} %param.7) | copy-start | bytes 393220
  111.1 187.5 %all-gather.3.cloned.1.call-start = ((), (), s32[]{:S(2)}) async-start(), calls=%async_computation.2 | async-start | bytes 4325376 | tf_op jit(solution)/shard_map/all_gather | solution.py:35
  235.7 184.3 %reduce-scatter.3.cloned.1.call-start = ((), (), s32[]{:S(2)}) async-start(), calls=%async_computation.3 | async-start | bytes 1179648 | tf_op jit(solution)/shard_map/reduce_scatter | solution.py:41
Sparse Core Ops, SparseCore 0:
  11.2 55.0 all-gather.4
  111.2 122.7 reduce-scatter.4
  236.4 62.1 all-gather.2
  342.2 77.7 reduce-scatter.2
where the time goes:
time: 429 us; the launch traced here: 428 us
  waiting for transfers between devices  318 us (74%)
  matrix products  51.9 us (12%)
  local copies, waits for them, and re-layouts  37.1 us (9%)
  between operations  14.5 us (3%)
  other arithmetic  7.09 us (2%)
    reduce_scatter x1, waiting for transfers between devices, per_device(): lax.psum_scatter(backward.reshape(-1, feature_width), 'col', scatter_dime...  123 us
    reduce_scatter x1, waiting for transfers between devices, per_device(): lax.psum_scatter(forward.reshape(-1, feature_width), 'row', scatter_dimen...  77.9 us
    all_gather x1, waiting for transfers between devices, per_device(): embed_panel = lax.all_gather(scaled, 'col', axis=0, tiled=True)  62.9 us
    all_gather x1, waiting for transfers between devices, per_device(): grad_panel = lax.all_gather(grad_scaled, 'row', axis=0, tiled=True)  53.9 us
    dot_general x1, matrix products, tile_terms(): jnp.einsum('tij,tjd->tid', values, picked, precision=lax.Precision.HIGHEST)  21.2 us
    dot_general x1, matrix products, tile_terms(): jnp.einsum('tij,tid->tjd', values, grad_picked, precision=lax.Precision.H...  19.5 us
    dot_general x1, local copies, waits for them, and re-layouts, tile_terms(): jnp.einsum('tij,tid->tjd', values, grad_picked, precision=lax.Precision.H...  9.36 us
    dot_general x1, local copies, waits for them, and re-layouts, tile_terms(): jnp.einsum('tij,tjd->tid', values, picked, precision=lax.Precision.HIGHEST)  9.36 us
  transfers between devices with their start and end apart: 4, of which 4 were waited for; matrix products, arithmetic and copies ran while one was open for 0% of the time, Pallas kernels for 0%

commit v1 on v0

--- a/solution.py
+++ b/solution.py
@@ -33,7 +33,9 @@
     scaled = embed * lax.rsqrt(col_degree.astype(jnp.float32))[:, None]
     grad_scaled = cotangent * lax.rsqrt(row_degree.astype(jnp.float32))[:, None]
     embed_panel = lax.all_gather(scaled, "col", axis=0, tiled=True)
-    grad_panel = lax.all_gather(grad_scaled, "row", axis=0, tiled=True)
+    grad_panel = jnp.concatenate(
+        lax.all_to_all(jnp.stack([grad_scaled] * lax.axis_size("row")), "row", 0, 0), axis=0
+    )
     panel_tiles = embed_panel.reshape(-1, tile_size, feature_width)
     grad_tiles = grad_panel.reshape(-1, tile_size, feature_width)
     live_mask = jnp.arange(capacity, dtype=jnp.int32) < live_count

time: 429 us -> 395 us (0.921)
  waiting for transfers between devices: 318 us -> 278 us
  starting transfers between devices: 0.16 us -> 7.55 us
    all_gather x1 -> x0, waiting for transfers between devices: 53.9 us -> none  [per_device(): grad_panel = lax.all_gather(grad_scaled, 'row', axis=0, tiled=True)]
    all_to_all x0 -> x1, waiting for transfers between devices: none -> 11.8 us  [per_device(): lax.all_to_all(jnp.stack([grad_scaled] * lax.axis_size('row')), 'row', 0, 0)]
    all_to_all x0 -> x1, starting transfers between devices: none -> 7.46 us  [per_device(): lax.all_to_all(jnp.stack([grad_scaled] * lax.axis_size('row')), 'row', 0, 0)]
  transfers between devices with their start and end apart: 4 -> 4, of which waited for: 4 -> 4; matrix products, arithmetic and copies ran while one was open for 0% -> 1% of each run, Pallas kernels for 0% -> 0%
where the time goes in v1:
time: 395 us
  waiting for transfers between devices  278 us (70%)
  matrix products  51.9 us (13%)
  local copies, waits for them, and re-layouts  36.8 us (9%)
  between operations  14.5 us (4%)
  starting transfers between devices  7.55 us (2%)
  other arithmetic  6.43 us (2%)
    reduce_scatter x1, waiting for transfers between devices, per_device(): lax.psum_scatter(backward.reshape(-1, feature_width), 'col', scatter_dime...  125 us
    reduce_scatter x1, waiting for transfers between devices, per_device(): lax.psum_scatter(forward.reshape(-1, feature_width), 'row', scatter_dimen...  77.8 us
    all_gather x1, waiting for transfers between devices, per_device(): embed_panel = lax.all_gather(scaled, 'col', axis=0, tiled=True)  63.3 us
    dot_general x1, matrix products, tile_terms(): jnp.einsum('tij,tjd->tid', values, picked, precision=lax.Precision.HIGHEST)  21.2 us
    dot_general x1, matrix products, tile_terms(): jnp.einsum('tij,tid->tjd', values, grad_picked, precision=lax.Precision.H...  19.5 us
    all_to_all x1, waiting for transfers between devices, per_device(): lax.all_to_all(jnp.stack([grad_scaled] * lax.axis_size('row')), 'row', 0, 0)  11.8 us
    dot_general x1, local copies, waits for them, and re-layouts, tile_terms(): jnp.einsum('tij,tjd->tid', values, picked, precision=lax.Precision.HIGHEST)  9.31 us
    dot_general x1, local copies, waits for them, and re-layouts, tile_terms(): jnp.einsum('tij,tid->tjd', values, grad_picked, precision=lax.Precision.H...  9.26 us
  transfers between devices with their start and end apart: 4, of which 4 were waited for; matrix products, arithmetic and copies ran while one was open for 1% of the time, Pallas kernels for 0%

profile of v1, /device:TPU:2, one launch (start us, length us, event | category | flops | bytes accessed | tf_op | source)
XLA Modules:
  0.0 394.7 jit_solution(3444113678193743025)
XLA Ops:
  7.2 0.7 convert_rsqrt_fusion
  7.8 1.0 broadcast_multiply_fusion
  8.9 1.0 stack.2
  9.9 7.5 %all-to-all-start = ((f32[8,256,128]{2,1,0:T(8,128)}), f32[8,256,128]{2,1,0:T(8,128)S(1)}, u32[]{:S(2)}, u32[]{:S(2)}) async-start(f32[8,256,128]{2,1,0:T(8,128)} %stack.2), calls=%async_computation.1 | async-start | bytes 2097152 | tf_op jit(solution)/shard_map/all_to_all | solution.py:37
  17.4 0.0 reduce-scatter.5.cloned.1.call-start
  18.0 0.7 fusion.25
  18.7 0.7 slice_bitcast_fusion
  19.4 0.7 compare_and_fusion
  20.1 11.8 %all-to-all-done = f32[8,256,128]{2,1,0:T(8,128)S(1)} async-done(((f32[8,256,128]{2,1,0:T(8,128)}), f32[8,256,128]{2,1,0:T(8,128)S(1)}, u32[]{:S(2)}, u32[]{:S(2)}) %all-to-all-start) | async-done | bytes 1048608 | tf_op jit(solution)/shard_map/all_to_all | solution.py:37
  31.9 4.3 %gather_fusion.1 = f32[128,128,128]{2,1,0:T(8,128)} fusion(f32[16,128,128]{2,1,0:T(8,128)S(1)} %bitcast.39, s32[1024]{0:T(1024)S(1)} %pad_clamp_fusion), kind=kCustom, calls=%fused_computation.1 | custom fusion | bytes 16777728 | tf_op jit(solution)/shard_map/jit(_take)/gather | solution.py:15
  36.2 19.5 %fusion.4 = f32[128,128,128]{2,1,0:T(8,128)} fusion(f32[1,1,128,128,128]{4,3,2,1,0:T(8,128)} %param.9, f32[128,128,128]{2,1,0:T(8,128)} %gather_fusion.1, pred[128]{0:T(512)(128)(4,1)S(1)} %get-tuple-element.6), kind=kOutput, calls=%fused_computation.6 | convolution fusion | flops 3223322624 | bytes 25165952 | tf_op jit(solution)/shard_map/tij,tid->tjd/dot_general | solution.py:16
  55.7 9.3 %copy.12 = f32[128,128,128]{1,0,2:T(8,128)} copy(f32[128,128,128]{2,1,0:T(8,128)} %fusion.4) | data formatting | bytes 16777216 | tf_op jit(solution)/shard_map/tij,tid->tjd/dot_general | solution.py:16
  65.0 6.0 %fusion = f32[64,128,128]{2,0,1:T(8,128)S(1)} fusion(f32[128,128,128]{1,0,2:T(8,128)} %copy.12, s32[128]{0:T(128)S(1)} %get-tuple-element.4, pred[128]{0:T(512)(128)(4,1)S(1)} %iota_compare_fusion.2), kind=kOutput, calls=%fused_computation.2 | convolution fusion | flops 1610629120 | bytes 12583552 | tf_op jit(solution)/shard_map/bt,tjd->bjd/dot_general | solution.py:21
  71.0 0.0 copy-start.1
  71.0 0.0 copy-start
  71.1 4.4 %copy.10 = f32[64,128,128]{2,1,0:T(8,128)} copy(f32[64,128,128]{2,0,1:T(8,128)S(1)} %fusion) | data formatting | bytes 8388608 | tf_op jit(solution)/shard_map/bt,tjd->bjd/dot_general | solution.py:21
  75.4 0.0 reduce-scatter.5.cloned.1.call-update
  75.5 0.0 all-gather.2.cloned.1.call-start
  75.5 0.0 copy-done.1
  75.5 124.6 %reduce-scatter.5.cloned.1.call-done = f32[256,128]{1,0:T(8,128)} async-done(((f32[8192,128]{1,0:T(8,128)}), f32[256,128]{1,0:T(8,128)}) %reduce-scatter.5.cloned.1.call-update) | async-done | bytes 131088 | tf_op jit(solution)/shard_map/reduce_scatter | solution.py:47
  200.1 0.0 copy-done
  200.1 1.7 broadcast_multiply_fusion.2
  201.8 0.0 all-gather.2.cloned.1.call-update
  201.9 0.0 reduce-scatter.3.cloned.1.call-start
  201.9 63.3 %all-gather.2.cloned.1.call-done = f32[8192,128]{1,0:T(8,128)} async-done(((f32[256,128]{1,0:T(8,128)}), f32[8192,128]{1,0:T(8,128)}) %all-gather.2.cloned.1.call-update) | async-done | bytes 4194320 | tf_op jit(solution)/shard_map/all_gather | solution.py:35
  265.2 6.5 %gather_fusion = f32[128,128,128]{2,1,0:T(8,128)} fusion(f32[64,128,128]{2,1,0:T(8,128)} %bitcast.40, s32[1024]{0:T(1024)S(1)} %pad_clamp_fusion.1), kind=kCustom, calls=%fused_computation | custom fusion | bytes 16777728 | tf_op jit(solution)/shard_map/jit(_take)/gather | solution.py:8
  271.7 21.2 %fusion.6 = f32[128,128,128]{2,1,0:T(8,128)} fusion(f32[1,1,128,128,128]{4,3,2,1,0:T(8,128)} %param.9, f32[128,128,128]{2,1,0:T(8,128)} %gather_fusion, pred[128]{0:T(512)(128)(4,1)S(1)} %get-tuple-element.7), kind=kOutput, calls=%fused_computation.8 | convolution fusion | flops 3223322624 | bytes 25165952 | tf_op jit(solution)/shard_map/tij,tjd->tid/dot_general | solution.py:9
  292.9 9.3 %copy.11 = f32[128,128,128]{1,0,2:T(8,128)} copy(f32[128,128,128]{2,1,0:T(8,128)} %fusion.6) | data formatting | bytes 16777216 | tf_op jit(solution)/shard_map/tij,tjd->tid/dot_general | solution.py:9
  302.2 5.2 %fusion.2 = f32[16,128,128]{2,0,1:T(8,128)S(1)} fusion(f32[128,128,128]{1,0,2:T(8,128)} %copy.11, s32[128]{0:T(128)S(1)} %get-tuple-element.5, pred[128]{0:T(512)(128)(4,1)S(1)} %iota_compare_fusion.2), kind=kOutput, calls=%fused_computation.4 | convolution fusion | flops 402657280 | bytes 9437824 | tf_op jit(solution)/shard_map/at,tid->aid/dot_general | solution.py:14
  307.4 1.3 copy.9
  308.7 0.0 reduce-scatter.3.cloned.1.call-update
  308.7 77.8 %reduce-scatter.3.cloned.1.call-done = f32[256,128]{1,0:T(8,128)} async-done(((f32[2048,128]{1,0:T(8,128)}), f32[256,128]{1,0:T(8,128)}) %reduce-scatter.3.cloned.1.call-update) | async-done | bytes 131088 | tf_op jit(solution)/shard_map/reduce_scatter | solution.py:43
  386.5 1.7 broadcast_multiply_fusion.1
  (4 shorter events, 0.0 us)
Async XLA Ops:
  9.9 22.0 %all-to-all-start = ((f32[8,256,128]{2,1,0:T(8,128)}), f32[8,256,128]{2,1,0:T(8,128)S(1)}, u32[]{:S(2)}, u32[]{:S(2)}) async-start(f32[8,256,128]{2,1,0:T(8,128)} %stack.2), calls=%async_computation.1 | async-start | bytes 2097152 | tf_op jit(solution)/shard_map/all_to_all | solution.py:37
  17.4 182.8 %reduce-scatter.5.cloned.1.call-start = ((), (), s32[]{:S(2)}) async-start(), calls=%async_computation.5 | async-start | bytes 4325376 | tf_op jit(solution)/shard_map/reduce_scatter | solution.py:47
  71.0 4.5 %copy-start.1 = (s32[256]{0:T(256)S(1)}, s32[256]{0:T(256)}, u32[]{:S(2)}) copy-start(s32[256]{0:T(256)} %param.13) | copy-start | bytes 3076
  71.0 129.1 %copy-start = (f32[256,128]{1,0:T(8,128)S(1)}, f32[256,128]{1,0:T(8,128)}, u32[]{:S(2)}) copy-start(f32[256,128]{1,0:T(8,128)} %param.7) | copy-start | bytes 393220
  75.5 189.7 %all-gather.2.cloned.1.call-start = ((), (), s32[]{:S(2)}) async-start(), calls=%async_computation.3 | async-start | bytes 4325376 | tf_op jit(solution)/shard_map/all_gather | solution.py:35
  201.9 184.7 %reduce-scatter.3.cloned.1.call-start = ((), (), s32[]{:S(2)}) async-start(), calls=%async_computation.4 | async-start | bytes 1179648 | tf_op jit(solution)/shard_map/reduce_scatter | solution.py:43
Sparse Core Ops, SparseCore 0:
  75.6 124.5 reduce-scatter.4
  202.6 62.5 all-gather.1
  308.8 77.6 reduce-scatter.2
